TPU v7x, 256 devices: a whole 4x4x8 slice. The times are simulated.
256 devices in a mesh: head: 4 (over x), grp: 4 (over y_hi, core), blk: 16 (over y_lo, z).
Axes of the slice: x: 4, y: 4 (y_hi: 2, y_lo: 2; y = y_hi * 2 + y_lo), z: 8, core: 2. Of those that a mesh axis runs over, the one named last changes fastest.
Arguments:
- tokens: bfloat16 [16384, 2880], P(('grp', 'blk'), 'head'), may hold values from -450 to 450
- norm_gain: float32 [2880], replicated, may hold values from 0.9 to 12
- w_query: bfloat16 [2880, 4096], P(None, 'head'), may hold values from -0.109375 to 0.109375
- w_key: bfloat16 [2880, 512], P(None, 'head'), may hold values from -0.109375 to 0.109375
- w_value: bfloat16 [2880, 512], P(None, 'head'), may hold values from -0.109375 to 0.109375
- sinks: float32 [64], P('head'), may hold values from 0 to 8
- doc_lengths: int32 [12], replicated, may hold values from 1 to 8192, 16384 in all
- tile_mask: int32 [128, 128], replicated, may hold values 0 or 1
Outputs:
- attended: bfloat16 [16384, 4096], P(('grp', 'blk'), 'head')
Inputs may be any that keep to these rules, and one draw needn't show every extreme that they name: `doc_lengths`: the 12 lengths sum to 16384 and the longest is exactly 8192.
All inputs are finite; a program needn't handle non-finite values.
Results may differ from a plain program's by a relative error of at most 0.017.
The roundings to bfloat16 on the way count: a program that leaves them out, or rounds other values in their place, can miss the bound.
Values may be sent and summed in bfloat16 or wider, within the bound.
A program may use at most 64 MiB of HBM per device.

v0:
```python
import functools

import jax
import jax.numpy as jnp
from jax import lax
from jax.experimental import pallas as pl
from jax.experimental.pallas import tpu as pltpu
from jax.sharding import PartitionSpec as P

MESH = pl.DeviceIdType.MESH
HD = 64
TILE = 128
ROWS = 256
NT = 128
CH = 4
EPS = 1e-05
ROPE_BASE = 150000.0
LOG2E = 1.4426950408889634
ORDER = (
    (0, -1, 0),
    (0, 0, -1),
    (0, 0, 1),
    (0, 1, 0),
    (1, -1, 0),
    (1, 0, -1),
    (1, 0, 1),
    (1, 1, 0),
    (0, 0, -2),
    (0, 0, 2),
    (0, 1, -1),
    (0, 2, 0),
    (0, -1, -1),
    (0, 1, 1),
    (1, -1, -1),
    (1, -1, 1),
    (0, -1, 1),
    (1, 0, -2),
    (1, 0, 2),
    (0, 1, -2),
    (1, 1, -1),
    (1, 1, 1),
    (1, 2, 0),
    (0, 1, 2),
    (0, -1, -2),
    (0, 0, -3),
    (0, 0, 3),
    (0, 2, -1),
    (0, -1, 2),
    (1, -1, -2),
    (1, -1, 2),
    (0, 2, 1),
    (1, 0, -3),
    (1, 0, 3),
    (0, 1, -3),
    (0, 2, -2),
    (1, 1, -2),
    (1, 1, 2),
    (0, -1, -3),
    (0, 1, 3),
    (1, 2, -1),
    (1, 2, 1),
    (0, -1, 3),
    (0, 2, -3),
    (0, 0, -4),
    (1, -1, 3),
    (0, 2, 2),
    (0, 2, 3),
    (1, -1, -3),
    (1, 1, 3),
    (1, 0, -4),
    (1, 2, 2),
    (0, -1, -4),
    (0, 1, -4),
    (1, 1, -3),
    (1, 1, 4),
    (1, 2, -2),
    (1, 2, 3),
    (0, 2, -4),
    (1, -1, -4),
    (1, 2, -3),
    (1, 2, 4),
)
BF = jnp.bfloat16
F32 = jnp.float32

def place():
    h = lax.axis_index("head")
    g = lax.axis_index("grp")
    b = lax.axis_index("blk")
    c = g % 2
    y = (g // 2) * 2 + b // 8
    z = b % 8
    return h, c, y, z


def device(yy, zz, core):
    return {"grp": (yy // 2) * 2 + core, "blk": (yy % 2) * 8 + zz}


def shard_id(yy, zz, core):
    return (yy // 2) * 32 + core * 16 + (yy % 2) * 8 + zz


class Swap:
    def __init__(self, src, dst, relay, sems, c, y, z):
        self.src, self.dst, self.relay = src, dst, relay
        self.s_sem, self.r_sem, self.q_sem = sems
        self.c, self.y, self.z = c, y, z
        self.me = c * 4 + y
        self.up, self.down, self.far = (y + 1) % 4, (y + 3) % 4, (y + 2) % 4
        self.sent = []

    def go(self, src, dst, r_sem, target):
        cp = pltpu.make_async_remote_copy(
            src, dst, self.s_sem.at[len(self.sent)], r_sem, device_id=target, device_id_type=MESH)
        cp.start()
        self.sent.append(cp)

    def await_at(self, dst, r_sem):
        pltpu.make_async_remote_copy(
            dst, dst, self.s_sem.at[0], r_sem,
            device_id=device(self.y, self.z, 1 - self.c), device_id_type=MESH).wait_recv()

    def start(self):
        c, z, me = self.c, self.z, self.me
        self.go(self.src(self.far), self.relay.at[0], self.q_sem.at[0], device(self.up, z, c))
        self.go(self.src(4 + self.far), self.relay.at[1], self.q_sem.at[1], device(self.down, z, c))
        for core in range(2):
            self.go(self.src(core * 4 + self.up), self.dst(me), self.r_sem.at[me], device(self.up, z, core))
            self.go(self.src(core * 4 + self.down), self.dst(me), self.r_sem.at[me], device(self.down, z, core))
        self.go(self.src((1 - c) * 4 + self.y), self.dst(me), self.r_sem.at[me], device(self.y, z, 1 - c))

    def forward(self):
        c, z = self.c, self.z
        below, above = c * 4 + self.down, c * 4 + self.up
        self.await_at(self.relay.at[0], self.q_sem.at[0])
        self.go(self.relay.at[0], self.dst(below), self.r_sem.at[below], device(self.up, z, 0))
        self.await_at(self.relay.at[1], self.q_sem.at[1])
        self.go(self.relay.at[1], self.dst(above), self.r_sem.at[above], device(self.down, z, 1))

    def finish(self):
        for d in range(1, 8):
            i = (self.me + d) % 8
            self.await_at(self.dst(i), self.r_sem.at[i])
        for cp in self.sent:
            cp.wait_send()


def turned(x, cos, sin):
    lane = lax.broadcasted_iota(jnp.int32, x.shape, 1)
    other = jnp.where(lane % 64 < 32, pltpu.roll(x, 96, 1), pltpu.roll(x, 32, 1))
    return x * cos + other * sin


def angles(base):
    lane = lax.broadcasted_iota(jnp.int32, (1, 128), 1)
    freq = jnp.zeros((1, 128), F32)
    for i in range(HD // 2):
        freq = jnp.where(lane % 32 == i, ROPE_BASE ** (-2.0 * i / HD), freq)
    pos = lax.broadcasted_iota(jnp.int32, (ROWS, 128), 0) + base
    ang = pos.astype(F32) * freq
    sin = jnp.sin(ang)
    return jnp.cos(ang), jnp.where(lane % 64 < 32, -sin, sin)


def doc_start(doc_len, pos):
    end = jnp.int32(0)
    first = jnp.zeros_like(pos)
    for d in range(doc_len.shape[0]):
        end = end + doc_len[d]
        first = jnp.maximum(first, jnp.where(end <= pos, end, 0))
    return first


def key_lists(doc_len, tile_mask, z, lists):
    n = lax.broadcasted_iota(jnp.int32, (1, 128), 1)
    i = n // 2
    yy, core = i % 4, i // 4
    tile = shard_id(yy, z, core) * 2 + n % 2
    first = doc_start(doc_len, tile * TILE)
    last = doc_start(doc_len, tile * TILE + TILE - 1)
    j = lax.broadcasted_iota(jnp.int32, (NT, 128), 0)
    k = lax.broadcasted_iota(jnp.int32, (NT, 128), 1)
    pick = jnp.where(j == tile, 1.0, 0.0).astype(BF)
    listed = jnp.dot(tile_mask[...].astype(F32).T.astype(BF), pick, preferred_element_type=F32) > 0.5
    active = (listed | (j == tile)) & (j <= tile) & (j * TILE + TILE > first)
    act = jnp.where(active, 1.0, 0.0).astype(BF)
    lower = jnp.where(k < j, 1.0, 0.0).astype(BF)
    before = jnp.dot(lower, act, preferred_element_type=F32).astype(jnp.int32)
    spot = jnp.where(active, jnp.where(j == tile, 0, before + 1), -1)
    count = jnp.sum(jnp.where(active, 1, 0), axis=0, keepdims=True)
    for r in range(16):
        hit = spot[:, r:r + 1] == k
        lists[r:r + 1, :] = jnp.sum(jnp.where(hit, j - NT, 0), axis=0, keepdims=True) + NT
    lists[16:17, :] = tile
    lists[17:18, :] = (count + CH - 1) // CH
    lists[18:19, :] = jnp.where(first == last, 0, 1)
    lists[19:24, :] = jnp.zeros((5, 128), jnp.int32)


def project_kernel(
    doc_len, tok_hbm, gain_hbm, mask_hbm, wq_hbm, wk_hbm, wv_hbm,
    kv_out, q_out, lists,
    xt, xb, gain, mask, wq, wkv, kvs, kvb, kvu, qs, relay,
    wsem, xs_sem, xr_sem, ks_sem, kr_sem, ps_sem, us_sem, qs_sem, qr_sem, qq_sem,
):
    h, c, y, z = place()
    me = c * 4 + y
    feats = xb.shape[2]
    half = ROWS // 2

    copies = [
        pltpu.make_async_copy(tok_hbm, xt.at[h], wsem.at[0]),
        pltpu.make_async_copy(gain_hbm, gain.at[0], wsem.at[1]),
        pltpu.make_async_copy(mask_hbm, mask, wsem.at[2]),
        pltpu.make_async_copy(wk_hbm, wkv.at[:, 0:128], wsem.at[3]),
        pltpu.make_async_copy(wv_hbm, wkv.at[:, 128:256], wsem.at[4]),
        pltpu.make_async_copy(wq_hbm, wq, wsem.at[5]),
    ]
    for cp in copies:
        cp.start()

    def plane(dy, dz):
        return device((y + dy + 4) % 4, (z + dz + 8) % 8, c)

    def mate(d):
        i = (me + d) % 8
        return i, device(i % 4, z, i // 4)

    partner = device(y, z, 1 - c)
    ahead, behind, across = (h + 1) % 4, (h + 3) % 4, (h + 2) % 4
    barrier = pltpu.get_barrier_semaphore()
    for x in (ahead, behind):
        pl.semaphore_signal(barrier, inc=1, device_id={"head": x}, device_id_type=MESH)
    for dz in (1, -1):
        pl.semaphore_signal(barrier, inc=1, device_id=plane(0, dz), device_id_type=MESH)
    for d in range(1, 8):
        pl.semaphore_signal(barrier, inc=1, device_id=mate(d)[1], device_id_type=MESH)
    pl.semaphore_wait(barrier, 11)
    copies[0].wait()

    xsent = []
    top, low = pl.ds(0, half), pl.ds(half, half)

    def xsend(n, src, rows, to):
        cp = pltpu.make_async_remote_copy(
            xt.at[src, :, rows], xt.at[src, :, rows], xs_sem.at[n], xr_sem.at[n],
            device_id={"head": to}, device_id_type=MESH)
        cp.start()
        xsent.append(cp)

    def xwait(n, src, rows):
        pltpu.make_async_remote_copy(
            xt.at[src, :, rows], xt.at[src, :, rows], xs_sem.at[n], xr_sem.at[n],
            device_id={"head": ahead}, device_id_type=MESH).wait_recv()

    xsend(0, h, top, ahead)
    xsend(1, h, low, behind)
    xsend(2, h, low, ahead)
    xsend(3, h, top, behind)
    cos, sin = angles(shard_id(y, z, c) * ROWS)
    xwait(0, behind, top)
    xsend(4, behind, top, ahead)
    xwait(1, ahead, low)
    xsend(5, ahead, low, behind)

    copies[2].wait()
    key_lists(doc_len, mask, z, lists)
    kvu[64] = jnp.zeros((2, 208, 128), BF)
    copies[1].wait()

    def squares(i):
        w = xt[i].astype(F32).T
        xb[i] = w.astype(BF)
        return jnp.sum(w * w, axis=1, keepdims=True)

    total = squares(h)
    xwait(2, behind, low)
    total = total + squares(behind)
    xwait(3, ahead, top)
    total = total + squares(ahead)
    xwait(4, across, top)
    xwait(5, across, low)
    total = total + squares(across)
    scale = lax.rsqrt(total / (4 * feats) + EPS)
    for cp in xsent:
        cp.wait_send()
    copies[3].wait()
    copies[4].wait()
    kvp = jnp.zeros((ROWS, 256), F32)
    for i in range(4):
        w = xb[i].astype(F32) * scale * gain[:, i * feats:(i + 1) * feats]
        w = w.astype(BF)
        xb[i] = w
        kvp = kvp + jnp.dot(w, wkv[i * feats:(i + 1) * feats, :], preferred_element_type=F32)
    k = turned(kvp[:, :128], cos, sin)
    v = kvp[:, 128:]
    lane = lax.broadcasted_iota(jnp.int32, (64, 128), 1)
    for e in range(2):
        k0, k1 = k[128 * e:128 * e + 64], k[128 * e + 64:128 * e + 128]
        vt = v[128 * e:128 * (e + 1)].T.astype(BF)
        kvs[0, 128 * e:128 * e + 64, :] = jnp.where(lane < 64, k0, pltpu.roll(k1, 64, 1)).astype(BF)
        kvs[1, 128 * e:128 * e + 64, :] = jnp.where(lane < 64, pltpu.roll(k0, 64, 1), k1).astype(BF)
        for cc in range(2):
            kvs[cc, 128 * e + 64:128 * e + 128, :] = vt[64 * cc:64 * (cc + 1)]
    own = shard_id(y, z, c)
    other = shard_id(y, z, 1 - c)
    pcopy = pltpu.make_async_remote_copy(
        kvs.at[1 - c], kvb.at[own], ps_sem, kr_sem.at[own], device_id=partner, device_id_type=MESH)
    pcopy.start()
    kvb[own] = kvs[c]

    sends, outs = [], []
    null = pltpu.make_async_copy(kvu.at[64], kv_out.at[64], us_sem.at[64])
    null.start()
    outs.append(null)

    def send(sid, target):
        cp = pltpu.make_async_remote_copy(
            kvb.at[sid], kvb.at[sid], ks_sem.at[len(sends)], kr_sem.at[sid],
            device_id=target, device_id_type=MESH)
        cp.start()
        sends.append(cp)

    def arrived(sid):
        pltpu.make_async_remote_copy(
            kvb.at[sid], kvb.at[sid], ps_sem, kr_sem.at[sid],
            device_id=partner, device_id_type=MESH).wait_recv()

    def unpack(sid):
        for e in range(2):
            k2 = kvb[sid, 128 * e:128 * e + 64, :].astype(F32)
            r2 = pltpu.roll(k2, 64, 1)
            kvu[sid, e, 0:64, :] = jnp.where(lane < 64, k2, r2).astype(BF)
            kvu[sid, e, 64:128, :] = jnp.where(lane < 64, r2, k2).astype(BF)
            kvu[sid, e, 128:192, :] = kvb[sid, 128 * e + 64:128 * e + 128, :]
            kvu[sid, e, 192:208, :] = jnp.ones((16, 128), BF)
        cp = pltpu.make_async_copy(kvu.at[sid], kv_out.at[sid], us_sem.at[sid])
        cp.start()
        outs.append(cp)

    def block(dy, dz, core):
        return shard_id((y + dy + 4) % 4, (z + dz + 8) % 8, core)

    def q_block(n):
        acc = jnp.zeros((ROWS, 256), F32)
        for i in range(4):
            acc = acc + jnp.dot(
                xb[i], wq[i * feats:(i + 1) * feats, n * 256:(n + 1) * 256], preferred_element_type=F32)
        for u in range(2):
            qs[n * 2 + u] = (turned(acc[:, u * 128:(u + 1) * 128], cos, sin) * 0.125).astype(BF)

    for sid in (own, other):
        if sid is other:
            arrived(other)
        for dy, dz in ((0, 1), (0, -1), (1, 0), (-1, 0)):
            send(sid, plane(dy, dz))

    swap = Swap(lambda i: qs.at[i], lambda m: q_out.at[m], relay, (qs_sem, qr_sem, qq_sem), c, y, z)
    copies[5].wait()
    q_block(0)
    fresh = [own, other]
    seen = set()
    for at, (part, dy, dz) in enumerate(ORDER):
        sid = block(dy, dz, part)
        arrived(sid)
        seen.add((part, dy, dz))
        low_z, high_z = (-4, 3) if part == 0 or dy in (0, -1) else (-3, 4)
        if part == 1 or dy == 0:
            if dz <= 0 and dz > low_z:
                send(sid, plane(0, 1))
            if dz >= 0 and dz < high_z:
                send(sid, plane(0, -1))
        if part == 0:
            if dy == 0:
                send(sid, plane(1, 0))
                send(sid, plane(-1, 0))
            elif dy == -1 and dz % 2 == 0:
                send(sid, plane(1, 0))
            elif dy == 1 and dz % 2 == 1:
                send(sid, plane(-1, 0))
        elif dz == 0 and dy in (1, -1) and (1, -dy, 0) in seen:
            sgn = 1 - 2 * c
            send(shard_id((y - sgn + 4) % 4, z, 1), plane(sgn, 0))
        fresh.append(sid)
        if at == 5:
            q_block(1)
        if at == 9:
            q_block(2)
        if at == 13:
            q_block(3)
            swap.start()
            q_out[me] = qs[me]
        if at == 26:
            swap.forward()
        if at > 14:
            for _ in range(2):
                if fresh:
                    unpack(fresh.pop(0))
    for sid in fresh:
        unpack(sid)
    swap.finish()
    for cp in outs:
        cp.wait()
    for cp in sends + [pcopy]:
        cp.wait_send()


def attend_kernel(
    meta, doc_len, sinks, q_ref, kv_hbm, o_ref,
    kv, qsel, mref, aref, buf0, buf1, buf2, buf3, steps, sem,
):
    load = pltpu.make_async_copy(kv_hbm, kv, sem)
    load.start()
    bufs = ((buf0, buf1), (buf2, buf3))
    _, c, y, _ = place()
    base = (c * 4 + y) * 2
    lane = lax.broadcasted_iota(jnp.int32, (1, 256), 1)
    sub = lax.broadcasted_iota(jnp.int32, (TILE, 256), 0)
    sink = jnp.where(lane < 128, sinks[base], sinks[base + 1]) * LOG2E

    def prep(n4, cr):
        for u in range(4):
            n = n4 * 4 + u
            qt = (q_ref[n >> 1, 128 * (u & 1):128 * (u & 1) + 128, :].astype(F32) * LOG2E).T
            qt = jnp.concatenate([qt[:64], qt[64:]], axis=1)
            hi = qt.astype(BF)
            lo = (qt - hi.astype(F32)).astype(BF)
            qsel[n] = jnp.concatenate([hi, lo], axis=0)
        return cr

    lax.fori_loop(0, 4, prep, 0)

    def clear(n, cr):
        mref[n] = sink
        aref[n] = jnp.concatenate([jnp.zeros((64, 256), F32), jnp.ones((16, 256), F32)], axis=0)
        return cr

    lax.fori_loop(0, 18, clear, 0)

    counts = []
    for s in range(2):
        def add(i, cr):
            n = i * 2 + s
            steps[s * 2, i] = n << 7

            def put(ci, k):
                steps[s * 2 + 1, k] = (n << 7) + ci * CH
                return k + 1

            return lax.fori_loop(1, meta[17, n], put, cr)

        counts.append(lax.fori_loop(0, 8, add, jnp.int32(0)))
        steps[s * 2, 8] = (16 + s) << 7
    most = (jnp.maximum(counts[0], counts[1]) + 1) & ~1
    for s in range(2):
        def fill(k, cr):
            steps[s * 2 + 1, k] = (16 + s) << 7
            return cr
        lax.fori_loop(counts[s], most + 1, fill, 0)
    totals = (jnp.int32(8), most)
    load.wait()

    def scores(s, kind, k):
        w = steps[s * 2 + kind, k]
        nn = (w >> 7) & 15
        c0 = w & 127
        js = [meta[nn, c0 + u] for u in range(CH)]
        ks = [kv[j >> 1, j & 1, 0:128, :] for j in js]
        return jnp.dot(jnp.concatenate(ks, axis=0), qsel[nn], preferred_element_type=F32)

    def absorb(s, kind, k, sc):
        w = steps[s * 2 + kind, k]
        n = w >> 7
        nn = n & 15
        c0 = w & 127
        js = [meta[nn, c0 + u] for u in range(CH)]
        vt = jnp.concatenate([kv[j >> 1, j & 1, 128:208, :] for j in js], axis=1)
        mx, acc = mref[n], aref[n]
        if kind == 0:
            qpos = meta[16, nn] * TILE + (lane & 127)
            first = doc_start(doc_len, qpos)
            inside = first > meta[16, nn] * TILE
            mx = jnp.where(inside, sink, mx)
            acc = jnp.where(inside, jnp.concatenate([jnp.zeros((64, 256), F32), jnp.ones((16, 256), F32)], axis=0), acc)
            parts = []
            for u in range(CH):
                part = sc[u * 128:(u + 1) * 128]
                off = js[u] * TILE
                ok = sub >= first - off
                if u == 0:
                    ok = ok & (sub <= qpos - off)
                parts.append(jnp.where(ok, part, -1e30))
            sc = jnp.concatenate(parts, axis=0)
        new = jnp.maximum(mx, jnp.max(sc, axis=0, keepdims=True))
        p = jnp.exp2(sc - new).astype(BF)
        alpha = jnp.exp2(mx - new)
        mref[n] = new
        aref[n] = acc * alpha + jnp.dot(vt, p, preferred_element_type=F32)

    for kind in (1, 0):
        for s in range(2):
            bufs[s][0][...] = scores(s, kind, 0)

        def it(k2, cr):
            for ph in range(2):
                k = k2 * 2 + ph
                for s in range(2):
                    bufs[s][1 - ph][...] = scores(s, kind, k + 1)
                    absorb(s, kind, k, bufs[s][ph][...])
            return cr

        lax.fori_loop(0, totals[kind] >> 1, it, 0)

    def fin(n2, cr):
        for u in range(2):
            a = aref[n2 * 2 + u]
            out = a[:64] / a[64:65]
            out = jnp.concatenate([out[:, :128], out[:, 128:]], axis=0)
            o_ref[n2, 128 * u:128 * u + 128, :] = out.T.astype(BF)
        return cr

    lax.fori_loop(0, 8, fin, 0)


def return_kernel(o_ref, out_ref, relay, s_sem, r_sem, q_sem):
    h, c, y, z = place()
    me = c * 4 + y
    barrier = pltpu.get_barrier_semaphore()
    for d in range(1, 8):
        i = (me + d) % 8
        pl.semaphore_signal(barrier, inc=1, device_id=device(i % 4, z, i // 4), device_id_type=MESH)
    pl.semaphore_wait(barrier, 7)

    def cols(m):
        return pl.ds(pl.multiple_of(m * 128, 128), 128)

    swap = Swap(lambda i: o_ref.at[i], lambda m: out_ref.at[:, cols(m)], relay, (s_sem, r_sem, q_sem), c, y, z)
    swap.start()
    out_ref[:, cols(me)] = o_ref[me]
    swap.forward()
    swap.finish()


def body(tokens, norm_gain, w_query, w_key, w_value, sinks, doc_lengths, tile_mask):
    vm = pl.BlockSpec(memory_space=pltpu.VMEM)
    anym = pl.BlockSpec(memory_space=pl.ANY)
    smem = pl.BlockSpec(memory_space=pltpu.SMEM)
    feats = tokens.shape[1]
    dma = pltpu.SemaphoreType.DMA
    kv, q, lists = pl.pallas_call(
        project_kernel,
        out_shape=(
            jax.ShapeDtypeStruct((65, 2, 208, 128), BF),
            jax.ShapeDtypeStruct((8, ROWS, 128), BF),
            jax.ShapeDtypeStruct((24, 128), jnp.int32),
        ),
        in_specs=[smem] + [anym] * 6,
        out_specs=(anym, vm, vm),
        scratch_shapes=[
            pltpu.VMEM((4, feats, ROWS), BF),
            pltpu.VMEM((4, ROWS, feats), BF),
            pltpu.VMEM((1, 4 * feats), F32),
            pltpu.VMEM((NT, NT), jnp.int32),
            pltpu.VMEM((4 * feats, 1024), BF),
            pltpu.VMEM((4 * feats, 256), BF),
            pltpu.VMEM((2, ROWS, 128), BF),
            pltpu.VMEM((64, ROWS, 128), BF),
            pltpu.VMEM((65, 2, 208, 128), BF),
            pltpu.VMEM((8, ROWS, 128), BF),
            pltpu.VMEM((2, ROWS, 128), BF),
            dma((6,)), dma((6,)), dma((6,)), dma((64,)), dma((64,)), dma, dma((65,)), dma((9,)), dma((8,)), dma((2,)),
        ],
        compiler_params=pltpu.CompilerParams(collective_id=0, has_side_effects=True),
        name="project",
    )(doc_lengths, tokens.T, norm_gain, tile_mask, w_query, w_key, w_value)
    o = pl.pallas_call(
        attend_kernel,
        out_shape=jax.ShapeDtypeStruct((8, ROWS, 128), BF),
        in_specs=[smem, smem, smem, vm, anym],
        out_specs=vm,
        scratch_shapes=[
            pltpu.VMEM((65, 2, 208, 128), BF),
            pltpu.VMEM((16, 128, 256), BF),
            pltpu.VMEM((18, 1, 256), F32),
            pltpu.VMEM((18, 80, 256), F32),
        ] + [pltpu.VMEM((CH * TILE, 256), F32)] * 4 + [pltpu.SMEM((4, 256), jnp.int32), dma],
        name="attend",
    )(lists, doc_lengths, sinks, q, kv)
    return pl.pallas_call(
        return_kernel,
        out_shape=jax.ShapeDtypeStruct((ROWS, 1024), BF),
        in_specs=[vm],
        out_specs=vm,
        scratch_shapes=[pltpu.VMEM((2, ROWS, 128), BF), dma((9,)), dma((8,)), dma((2,))],
        compiler_params=pltpu.CompilerParams(collective_id=1, has_side_effects=True),
        name="give_back",
    )(o)


def solution(mesh):
    in_specs = (
        P(("grp", "blk"), "head"),
        P(),
        P(None, "head"),
        P(None, "head"),
        P(None, "head"),
        P("head"),
        P(),
        P(),
    )
    out_specs = P(("grp", "blk"), "head")
    return jax.shard_map(body, mesh=mesh, in_specs=in_specs, out_specs=out_specs, check_vma=False)
```

profile of v0, /device:TPU:1, one launch (start us, length us, event | category | flops | bytes accessed | tf_op | source)
XLA Modules:
  0.0 97.5 jit_solution(12404882495498367907)
XLA Ops:
  0.0 63.3 %project.1 = (bf16[65,2,208,128]{3,2,1,0:T(8,128)(2,1)}, bf16[8,256,128]{2,1,0:T(8,128)(2,1)}, s32[24,128]{1,0:T(8,128)}) custom-call(s32[12]{0:T(128)} %doc_len.3, bf16[720,256]{1,0:T(8,128)(2,1)} %bitcast.1, f32[2880]{0:T(1024)} %gain_hbm.1, s32[128,128]{1,0:T(8,128)} %mask_hbm.1, bf16[2880,1024]{1,0:T(8,128)(2,1)} %wq_hbm.1, bf16[2880,128]{1,0:T(8,128)(2,1)} %wk_hbm.1, ...), custom_call_target="tpu_custom_call" | custom-call | tf_op jit(solution)/shard_map/project/pallas_call | solution.py:551
  63.3 18.4 %attend.1.o_ref = bf16[8,256,128]{2,1,0:T(8,128)(2,1)} custom-call(s32[24,128]{1,0:T(8,128)} %get-tuple-element.8.meta, s32[12]{0:T(128)} %doc_len.3, f32[16]{0:T(128)} %sinks.1, bf16[8,256,128]{2,1,0:T(8,128)(2,1)} %get-tuple-element.9.q_ref, bf16[65,2,208,128]{3,2,1,0:T(8,128)(2,1)} %get-tuple-element.10.kv_hbm), custom_call_target="tpu_custom_call" | custom-call | tf_op jit(solution)/shard_map/attend/pallas_call | solution.py:577
  81.7 13.9 %give_back.1 = bf16[256,1024]{1,0:T(8,128)(2,1)} custom-call(bf16[8,256,128]{2,1,0:T(8,128)(2,1)} %attend.1.o_ref), custom_call_target="tpu_custom_call" | custom-call | tf_op jit(solution)/shard_map/give_back/pallas_call | solution.py:590
  95.6 1.9 %copy.10 = bf16[256,1024]{1,0:T(8,128)(2,1)} copy(bf16[256,1024]{1,0:T(8,128)(2,1)} %give_back.1) | data formatting | bytes 1048576
where the time goes:
time: 98.1 us; the launch traced here: 97.5 us
  Pallas kernels  95.6 us (97%)
  local copies, waits for them, and re-layouts  1.87 us (2%)
    pallas_call x1, Pallas kernels, body(): pl.pallas_call(project_kernel, out_shape=(jax.ShapeDtypeStruct((65, 2, 20...  63.3 us
    pallas_call x1, Pallas kernels, body(): pl.pallas_call(attend_kernel, out_shape=jax.ShapeDtypeStruct((8, ROWS, 12...  18.4 us
    pallas_call x1, Pallas kernels, body(): pl.pallas_call(return_kernel, out_shape=jax.ShapeDtypeStruct((ROWS, 1024)...  13.9 us

commit v1 on v0

--- a/solution.py
+++ b/solution.py
@@ -16,69 +16,25 @@
 EPS = 1e-05
 ROPE_BASE = 150000.0
 LOG2E = 1.4426950408889634
-ORDER = (
-    (0, -1, 0),
-    (0, 0, -1),
-    (0, 0, 1),
-    (0, 1, 0),
-    (1, -1, 0),
-    (1, 0, -1),
-    (1, 0, 1),
-    (1, 1, 0),
-    (0, 0, -2),
-    (0, 0, 2),
-    (0, 1, -1),
-    (0, 2, 0),
-    (0, -1, -1),
-    (0, 1, 1),
-    (1, -1, -1),
-    (1, -1, 1),
-    (0, -1, 1),
-    (1, 0, -2),
-    (1, 0, 2),
-    (0, 1, -2),
-    (1, 1, -1),
-    (1, 1, 1),
-    (1, 2, 0),
-    (0, 1, 2),
-    (0, -1, -2),
-    (0, 0, -3),
-    (0, 0, 3),
-    (0, 2, -1),
-    (0, -1, 2),
-    (1, -1, -2),
-    (1, -1, 2),
-    (0, 2, 1),
-    (1, 0, -3),
-    (1, 0, 3),
-    (0, 1, -3),
-    (0, 2, -2),
-    (1, 1, -2),
-    (1, 1, 2),
-    (0, -1, -3),
-    (0, 1, 3),
-    (1, 2, -1),
-    (1, 2, 1),
-    (0, -1, 3),
-    (0, 2, -3),
-    (0, 0, -4),
-    (1, -1, 3),
-    (0, 2, 2),
-    (0, 2, 3),
-    (1, -1, -3),
-    (1, 1, 3),
-    (1, 0, -4),
-    (1, 2, 2),
-    (0, -1, -4),
-    (0, 1, -4),
-    (1, 1, -3),
-    (1, 1, 4),
-    (1, 2, -2),
-    (1, 2, 3),
-    (0, 2, -4),
-    (1, -1, -4),
-    (1, 2, -3),
-    (1, 2, 4),
+ACTIONS = (
+    (0, 0, 0, -1), (0, 0, 0, 1), (0, 1, -1, 0), (0, 1, 1, 0), (1, 0, 0, -1), (2, 0, 0, 1), (5, 1, -1, 0),
+    (4, 0, 0, -1), (1, 1, -1, 0), (2, 1, 1, 0), (6, 0, 0, 0), (6, 1, 0, 0), (1, 1, 1, 0), (2, 1, -1, 0),
+    (6, 0, 0, 0), (6, 1, 0, 0), (0, 1, 0, -1), (0, 1, 0, 1), (0, 0, -1, 0), (0, 0, 1, 0), (1, 1, 0, -1),
+    (2, 1, 0, 1), (6, 0, 0, 0), (6, 1, 0, 0), (6, 0, 0, 0), (6, 1, 0, 0), (0, 0, 0, -2), (0, 0, 0, 2),
+    (0, 1, 2, 0), (0, 0, 1, -1), (1, 0, 0, -2), (2, 1, 2, 0), (1, 1, 2, 0), (2, 0, 0, 2), (3, 0, 0, -2),
+    (4, 0, 0, 1), (0, 1, -1, -1), (0, 1, 1, 1), (1, 1, -1, -1), (2, 1, 1, 1), (3, 0, 0, 2), (4, 0, 0, -2),
+    (0, 1, 1, -1), (0, 1, -1, 1), (1, 1, 1, -1), (2, 1, -1, 1), (3, 0, 0, -1), (4, 0, 0, 2), (0, 1, 0, -2),
+    (0, 1, 0, 2), (3, 0, 0, 1), (0, 0, 0, -3), (0, 1, 2, 1), (1, 0, 0, -3), (2, 1, 2, 1), (4, 0, 0, -3),
+    (1, 1, 0, -2), (2, 1, 0, 2), (3, 0, -1, 0), (0, 1, 2, -1), (0, 0, 0, 3), (0, 0, -1, -2), (0, 0, 1, 1),
+    (4, 0, 0, 3), (1, 1, 2, -1), (3, 0, 0, -3), (4, 0, 1, -1), (0, 1, -1, -2), (0, 1, 1, 2), (0, 0, -1, 2),
+    (0, 0, 1, -2), (2, 1, 1, 2), (1, 1, -1, -2), (3, 0, 0, 3), (4, 0, 1, 1), (0, 1, 1, -2), (0, 1, -1, 2),
+    (0, 0, -1, -1), (0, 0, 1, 2), (2, 1, -1, 2), (1, 1, 1, -2), (0, 0, 0, -4), (0, 1, 2, 2), (0, 0, -1, 1),
+    (0, 0, 1, -3), (2, 1, 2, 2), (3, 0, 0, -4), (4, 0, 0, -4), (3, 0, -1, -2), (4, 0, 1, -3), (0, 1, 0, -3),
+    (0, 1, 0, 3), (0, 0, 2, 0), (0, 0, 1, 3), (1, 1, 0, -3), (3, 0, -1, 2), (4, 0, 1, 3), (0, 1, 2, -2),
+    (0, 1, 1, 3), (0, 0, -1, -3), (0, 0, 2, -1), (2, 1, 1, 3), (1, 1, 2, -2), (0, 1, -1, -3), (0, 1, -1, 3),
+    (0, 0, -1, 3), (0, 0, 2, 1), (1, 1, -1, -3), (0, 1, 1, -3), (0, 1, 2, 3), (0, 0, -1, -4), (0, 0, 1, -4),
+    (2, 1, 2, 3), (3, 0, -1, -4), (0, 1, 0, -4), (0, 0, 2, -2), (0, 0, 2, -3), (0, 1, 1, 4), (0, 1, 2, -3),
+    (0, 0, 2, 2), (0, 0, 2, 3), (0, 1, -1, -4), (0, 1, 2, 4), (0, 0, 2, -4),
 )
 BF = jnp.bfloat16
 F32 = jnp.float32
@@ -121,14 +77,25 @@
             dst, dst, self.s_sem.at[0], r_sem,
             device_id=device(self.y, self.z, 1 - self.c), device_id_type=MESH).wait_recv()
 
+    def queue(self):
+        c, z, me = self.c, self.z, self.me
+        ups = [(self.far, self.relay.at[0], self.q_sem.at[0], device(self.up, z, c))]
+        downs = [(4 + self.far, self.relay.at[1], self.q_sem.at[1], device(self.down, z, c))]
+        for core in range(2):
+            ups.append((core * 4 + self.up, self.dst(me), self.r_sem.at[me], device(self.up, z, core)))
+            downs.append((core * 4 + self.down, self.dst(me), self.r_sem.at[me], device(self.down, z, core)))
+        self.side = ((1 - c) * 4 + self.y, self.dst(me), self.r_sem.at[me], device(self.y, z, 1 - c))
+        return ups, downs
+
+    def step(self, entry):
+        i, dst, r_sem, target = entry
+        self.go(self.src(i), dst, r_sem, target)
+
     def start(self):
-        c, z, me = self.c, self.z, self.me
-        self.go(self.src(self.far), self.relay.at[0], self.q_sem.at[0], device(self.up, z, c))
-        self.go(self.src(4 + self.far), self.relay.at[1], self.q_sem.at[1], device(self.down, z, c))
-        for core in range(2):
-            self.go(self.src(core * 4 + self.up), self.dst(me), self.r_sem.at[me], device(self.up, z, core))
-            self.go(self.src(core * 4 + self.down), self.dst(me), self.r_sem.at[me], device(self.down, z, core))
-        self.go(self.src((1 - c) * 4 + self.y), self.dst(me), self.r_sem.at[me], device(self.y, z, 1 - c))
+        for pair in zip(*self.queue()):
+            for entry in pair:
+                self.step(entry)
+        self.step(self.side)
 
     def forward(self):
         c, z = self.c, self.z
@@ -358,45 +325,32 @@
 
     swap = Swap(lambda i: qs.at[i], lambda m: q_out.at[m], relay, (qs_sem, qr_sem, qq_sem), c, y, z)
     copies[5].wait()
-    q_block(0)
+    for n in range(4):
+        q_block(n)
+    lines = swap.queue()
+    swap.step(swap.side)
+    q_out[me] = qs[me]
     fresh = [own, other]
-    seen = set()
-    for at, (part, dy, dz) in enumerate(ORDER):
+    waits = 0
+    for op, part, dy, dz in ACTIONS:
+        if op == 6:
+            if lines[part]:
+                swap.step(lines[part].pop(0))
+            continue
         sid = block(dy, dz, part)
-        arrived(sid)
-        seen.add((part, dy, dz))
-        low_z, high_z = (-4, 3) if part == 0 or dy in (0, -1) else (-3, 4)
-        if part == 1 or dy == 0:
-            if dz <= 0 and dz > low_z:
-                send(sid, plane(0, 1))
-            if dz >= 0 and dz < high_z:
-                send(sid, plane(0, -1))
-        if part == 0:
-            if dy == 0:
-                send(sid, plane(1, 0))
-                send(sid, plane(-1, 0))
-            elif dy == -1 and dz % 2 == 0:
-                send(sid, plane(1, 0))
-            elif dy == 1 and dz % 2 == 1:
-                send(sid, plane(-1, 0))
-        elif dz == 0 and dy in (1, -1) and (1, -dy, 0) in seen:
+        if op == 0:
+            arrived(sid)
+            fresh.append(sid)
+            waits += 1
+            if waits == 32:
+                swap.forward()
+            if waits > 12 and waits % 4 != 0:
+                unpack(fresh.pop(0))
+        elif op == 5:
             sgn = 1 - 2 * c
             send(shard_id((y - sgn + 4) % 4, z, 1), plane(sgn, 0))
-        fresh.append(sid)
-        if at == 5:
-            q_block(1)
-        if at == 9:
-            q_block(2)
-        if at == 13:
-            q_block(3)
-            swap.start()
-            q_out[me] = qs[me]
-        if at == 26:
-            swap.forward()
-        if at > 14:
-            for _ in range(2):
-                if fresh:
-                    unpack(fresh.pop(0))
+        else:
+            send(sid, plane(*((0, 1), (0, -1), (1, 0), (-1, 0))[op - 1]))
     for sid in fresh:
         unpack(sid)
     swap.finish()

time: 98.1 us -> 95.1 us (0.969); the launches traced: 97.5 us -> 95.6 us
  Pallas kernels: 95.6 us -> 93.7 us
    pallas_call x1, Pallas kernels: 63.3 us -> 60.2 us  [body(): pl.pallas_call(project_kernel, out_shape=(jax.ShapeDtypeStruct((65, 2, 20...]
    pallas_call x1, Pallas kernels: 18.4 us -> 21.2 us  [body(): pl.pallas_call(attend_kernel, out_shape=jax.ShapeDtypeStruct((8, ROWS, 12...]
    pallas_call x1, Pallas kernels: 13.9 us -> 12.2 us  [body(): pl.pallas_call(return_kernel, out_shape=jax.ShapeDtypeStruct((ROWS, 1024)...]
where the time goes in v1:
time: 95.1 us; the launch traced here: 95.6 us
  Pallas kernels  93.7 us (99%)
  local copies, waits for them, and re-layouts  1.87 us (2%)
    pallas_call x1, Pallas kernels, body(): pl.pallas_call(project_kernel, out_shape=(jax.ShapeDtypeStruct((65, 2, 20...  60.2 us
    pallas_call x1, Pallas kernels, body(): pl.pallas_call(attend_kernel, out_shape=jax.ShapeDtypeStruct((8, ROWS, 12...  21.2 us
    pallas_call x1, Pallas kernels, body(): pl.pallas_call(return_kernel, out_shape=jax.ShapeDtypeStruct((ROWS, 1024)...  12.2 us

profile of v1, /device:TPU:1, one launch (start us, length us, event | category | flops | bytes accessed | tf_op | source)
XLA Modules:
  0.0 95.6 jit_solution(12184064746238027215)
XLA Ops:
  0.0 60.2 %project.1 = (bf16[65,2,208,128]{3,2,1,0:T(8,128)(2,1)}, bf16[8,256,128]{2,1,0:T(8,128)(2,1)}, s32[24,128]{1,0:T(8,128)}) custom-call(s32[12]{0:T(128)} %doc_len.3, bf16[720,256]{1,0:T(8,128)(2,1)} %bitcast.1, f32[2880]{0:T(1024)} %gain_hbm.1, s32[128,128]{1,0:T(8,128)} %mask_hbm.1, bf16[2880,1024]{1,0:T(8,128)(2,1)} %wq_hbm.1, bf16[2880,128]{1,0:T(8,128)(2,1)} %wk_hbm.1, ...), custom_call_target="tpu_custom_call" | custom-call | tf_op jit(solution)/shard_map/project/pallas_call | solution.py:505
  60.2 21.2 %attend.1.o_ref = bf16[8,256,128]{2,1,0:T(8,128)(2,1)} custom-call(s32[24,128]{1,0:T(8,128)} %get-tuple-element.8.meta, s32[12]{0:T(128)} %doc_len.3, f32[16]{0:T(128)} %sinks.1, bf16[8,256,128]{2,1,0:T(8,128)(2,1)} %get-tuple-element.9.q_ref, bf16[65,2,208,128]{3,2,1,0:T(8,128)(2,1)} %get-tuple-element.10.kv_hbm), custom_call_target="tpu_custom_call" | custom-call | tf_op jit(solution)/shard_map/attend/pallas_call | solution.py:531
  81.5 12.2 %give_back.1 = bf16[256,1024]{1,0:T(8,128)(2,1)} custom-call(bf16[8,256,128]{2,1,0:T(8,128)(2,1)} %attend.1.o_ref), custom_call_target="tpu_custom_call" | custom-call | tf_op jit(solution)/shard_map/give_back/pallas_call | solution.py:544
  93.7 1.9 %copy.10 = bf16[256,1024]{1,0:T(8,128)(2,1)} copy(bf16[256,1024]{1,0:T(8,128)(2,1)} %give_back.1) | data formatting | bytes 1048576
